TPU v7x, 256 devices: a whole 4x4x8 slice. The times are simulated.
256 devices in a mesh: row: 16 (over x, y), col: 16 (over z, core).
Axes of the slice: x: 4, y: 4, z: 8, core: 2. Of those that a mesh axis runs over, the one named last changes fastest.
Arguments:
- features: bfloat16 [65536, 256], P(('col', 'row')), may hold values from -6 to 6
- cotangent: bfloat16 [65536, 256], P(('row', 'col')), may hold values from -1.5 to 1.5
- degrees: int32 [65536], P(('row', 'col')), may hold values from 8 to 40
- weight: bfloat16 [256, 256], replicated, may hold values from -0.375 to 0.375
- tile_rows: int32 [16, 16, 256], P('row', 'col'), may hold values from 0 to 31
- tile_cols: int32 [16, 16, 256], P('row', 'col'), may hold values from 0 to 31
- tile_bits: int32 [16, 16, 256, 16, 128], P('row', 'col'), may hold values from 0 to 255, as said below
- tile_count: int32 [16, 16], P('row', 'col'), may hold values from 16 to 256, as said below
Outputs:
- output: bfloat16 [65536, 256], P(('row', 'col'))
- weight_grad: float32 [256, 256], replicated
- input_grad: bfloat16 [65536, 256], P(('col', 'row'))
Inputs may be any that keep to these rules, and one draw needn't show every extreme that they name: `tile_bits`: each word holds 8 entries of 0 or 1 in its low bits; tiles at the same position may repeat and then add. `tile_count`: some device has all 256 slots live and some device 256 // 16.
All inputs are finite; a program needn't handle non-finite values.
Results may differ from a plain program's by a relative error of at most 0.024.
Values may be sent and summed in bfloat16 or wider, within the bound.
No kernel may reach another device: no remote copies, remote signals or barrier semaphores. Data moves between devices by JAX's collectives and lax.ppermute only.
A program may use at most 64 MiB of HBM per device.

v0:
```python
import math
import jax
import jax.numpy as jnp
from jax import lax
from jax.sharding import PartitionSpec as P


def unpack(packed):
    shifts = jnp.arange(8, dtype=jnp.int32)
    flags = jnp.right_shift(packed[:, :, None, :], shifts[None, None, :, None]) & 1
    return flags.reshape(packed.shape[0], packed.shape[1] * 8, packed.shape[2])


def sweep_tiles(packed, row_ids, col_ids, live_count, source, tile_offset, out_tiles, forward):
    tile_size = packed.shape[-1]
    feature_width = source.shape[-1]
    block_size = math.gcd(packed.shape[0], 32)

    def one_block(position, totals):
        offset = position * block_size
        block_bits = lax.dynamic_slice_in_dim(packed, offset, block_size, 0)
        block_rows = lax.dynamic_slice_in_dim(row_ids, offset, block_size, 0)
        block_cols = lax.dynamic_slice_in_dim(col_ids, offset, block_size, 0)
        if forward:
            target = block_rows - tile_offset
        else:
            target = block_cols - tile_offset
        inside = (target >= 0) & (target < out_tiles)
        live_mask = (offset + jnp.arange(block_size, dtype=jnp.int32) < live_count) & inside
        placed = jnp.clip(target, 0, out_tiles - 1)
        pattern = (unpack(block_bits) * live_mask.astype(jnp.int32)[:, None, None]).astype(
            jnp.bfloat16
        )
        if forward:
            product = jnp.einsum(
                "bji,bjf->bif", pattern, source[block_cols], preferred_element_type=jnp.float32
            )
        else:
            product = jnp.einsum(
                "bji,bif->bjf", pattern, source[block_rows], preferred_element_type=jnp.float32
            )
        return totals.at[placed].add(product)

    initial = jnp.zeros((out_tiles, tile_size, feature_width), jnp.float32)
    blocks_used = packed.shape[0] // block_size
    return lax.fori_loop(0, blocks_used, one_block, initial)


def forward_pass(features, degrees, weight, packed, row_ids, col_ids, live_count):
    tile_size = packed.shape[-1]
    width = features.shape[-1]
    gathered = lax.all_gather(features, "row", axis=0, tiled=True)
    source = gathered.reshape(-1, tile_size, width)
    out_tiles = features.shape[0] * lax.axis_size("col") // tile_size
    partial_value = sweep_tiles(packed, row_ids, col_ids, live_count, source, 0, out_tiles, True)
    summed = lax.psum_scatter(
        partial_value.reshape(-1, width).astype(jnp.bfloat16),
        "col",
        scatter_dimension=0,
        tiled=True,
    ).astype(jnp.float32)
    aggregated = (summed / degrees[:, None].astype(jnp.float32)).astype(jnp.bfloat16)
    output = jnp.dot(aggregated, weight, preferred_element_type=jnp.float32).astype(jnp.bfloat16)
    return (aggregated, output)


def backward_pass(cotangent, degrees, weight, packed, row_ids, col_ids, live_count):
    tile_size = packed.shape[-1]
    width = cotangent.shape[-1]
    scaled = (cotangent.astype(jnp.float32) / degrees[:, None].astype(jnp.float32)).astype(
        jnp.bfloat16
    )
    gathered = lax.all_gather(scaled, "col", axis=0, tiled=True)
    source = gathered.reshape(-1, tile_size, width)
    out_tiles = cotangent.shape[0] * lax.axis_size("row") // tile_size
    partial_value = sweep_tiles(packed, row_ids, col_ids, live_count, source, 0, out_tiles, False)
    summed = lax.psum_scatter(
        partial_value.reshape(-1, width).astype(jnp.bfloat16),
        "row",
        scatter_dimension=0,
        tiled=True,
    )
    return jnp.dot(summed, weight.T, preferred_element_type=jnp.float32).astype(jnp.bfloat16)


def per_device(features, cotangent, degrees, weight, tile_rows, tile_cols, tile_bits, tile_count):
    packed = tile_bits[0, 0]
    row_ids = tile_rows[0, 0]
    col_ids = tile_cols[0, 0]
    live_count = tile_count[0, 0]
    aggregated, output = forward_pass(
        features, degrees, weight, packed, row_ids, col_ids, live_count
    )
    input_grad = backward_pass(cotangent, degrees, weight, packed, row_ids, col_ids, live_count)
    local_term = lax.dot_general(
        aggregated, cotangent, (((0,), (0,)), ((), ())), preferred_element_type=jnp.float32
    )
    weight_grad = lax.psum(local_term, ("row", "col"))
    return (output, weight_grad, input_grad)


def solution(mesh):
    placed = (
        P(("col", "row"), None),
        P(("row", "col"), None),
        P(("row", "col")),
        P(),
        P("row", "col", None),
        P("row", "col", None),
        P("row", "col", None, None, None),
        P("row", "col"),
    )
    return jax.shard_map(
        per_device,
        mesh=mesh,
        in_specs=placed,
        out_specs=(P(("row", "col"), None), P(), P(("col", "row"), None)),
        check_vma=False,
    )
```

profile of v0, /device:TPU:2, one launch (start us, length us, event | category | flops | bytes accessed | tf_op | source)
XLA Modules:
  0.0 690.2 jit_solution(7609712674612229882)
XLA Ops:
  10.4 52.7 %all-gather.3.cloned.1.call-done = bf16[4096,256]{1,0:T(8,128)(2,1)} async-done(((bf16[256,256]{1,0:T(8,128)(2,1)}), bf16[4096,256]{1,0:T(8,128)(2,1)}) %all-gather.3.cloned.1.call-update) | async-done | bytes 2097168 | tf_op jit(solution)/shard_map/all_gather | solution.py:52
  65.5 136.1 %while.26 = (s32[]{:T(128)}, f32[32,128,256]{2,1,0:T(8,128)}, s32[256]{0:T(256)S(1)}, s32[256,16,128]{2,1,0:T(8,128)}, s32[]{:T(128)}, /*index=5*/s32[256]{0:T(2...) while((s32[]{:T(128)}, f32[32,128,256]{2,1,0:T(8,128)}, ...), condition=%wide.region_2.3_spmd, body=%wide.region_0.2_spmd.sunk | while | flops 271582656 | bytes 23862704 | solution.py:46
  72.6 10.0 %scatter_fusion = f32[32,128,256]{2,1,0:T(8,128)} fusion(f32[32,128,256]{2,1,0:T(8,128)} %get-tuple-element.398, s32[32]{0:T(128)S(1)} %get-tuple-element.375, f32[32,128,256]{2,1,0:T(8,128)} %fusion.35), kind=kCustom, calls=%fused_computation.2.clone.1 | custom fusion | flops 1048576 | bytes 12583040 | tf_op jit(solution)/shard_map/while/body/eval_jaxpr/scatter-add | solution.py:42
  89.7 10.0 %scatter_fusion = f32[32,128,256]{2,1,0:T(8,128)} fusion(f32[32,128,256]{2,1,0:T(8,128)} %get-tuple-element.398, s32[32]{0:T(128)S(1)} %get-tuple-element.375, f32[32,128,256]{2,1,0:T(8,128)} %fusion.35), kind=kCustom, calls=%fused_computation.2.clone.1 | custom fusion | flops 1048576 | bytes 12583040 | tf_op jit(solution)/shard_map/while/body/eval_jaxpr/scatter-add | solution.py:42
  106.8 9.8 %scatter_fusion = f32[32,128,256]{2,1,0:T(8,128)} fusion(f32[32,128,256]{2,1,0:T(8,128)} %get-tuple-element.398, s32[32]{0:T(128)S(1)} %get-tuple-element.375, f32[32,128,256]{2,1,0:T(8,128)} %fusion.35), kind=kCustom, calls=%fused_computation.2.clone.1 | custom fusion | flops 1048576 | bytes 12583040 | tf_op jit(solution)/shard_map/while/body/eval_jaxpr/scatter-add | solution.py:42
  123.6 9.9 %scatter_fusion = f32[32,128,256]{2,1,0:T(8,128)} fusion(f32[32,128,256]{2,1,0:T(8,128)} %get-tuple-element.398, s32[32]{0:T(128)S(1)} %get-tuple-element.375, f32[32,128,256]{2,1,0:T(8,128)} %fusion.35), kind=kCustom, calls=%fused_computation.2.clone.1 | custom fusion | flops 1048576 | bytes 12583040 | tf_op jit(solution)/shard_map/while/body/eval_jaxpr/scatter-add | solution.py:42
  140.6 9.9 %scatter_fusion = f32[32,128,256]{2,1,0:T(8,128)} fusion(f32[32,128,256]{2,1,0:T(8,128)} %get-tuple-element.398, s32[32]{0:T(128)S(1)} %get-tuple-element.375, f32[32,128,256]{2,1,0:T(8,128)} %fusion.35), kind=kCustom, calls=%fused_computation.2.clone.1 | custom fusion | flops 1048576 | bytes 12583040 | tf_op jit(solution)/shard_map/while/body/eval_jaxpr/scatter-add | solution.py:42
  157.5 10.0 %scatter_fusion = f32[32,128,256]{2,1,0:T(8,128)} fusion(f32[32,128,256]{2,1,0:T(8,128)} %get-tuple-element.398, s32[32]{0:T(128)S(1)} %get-tuple-element.375, f32[32,128,256]{2,1,0:T(8,128)} %fusion.35), kind=kCustom, calls=%fused_computation.2.clone.1 | custom fusion | flops 1048576 | bytes 12583040 | tf_op jit(solution)/shard_map/while/body/eval_jaxpr/scatter-add | solution.py:42
  171.7 2.9 fusion.35
  174.6 10.0 %scatter_fusion = f32[32,128,256]{2,1,0:T(8,128)} fusion(f32[32,128,256]{2,1,0:T(8,128)} %get-tuple-element.398, s32[32]{0:T(128)S(1)} %get-tuple-element.375, f32[32,128,256]{2,1,0:T(8,128)} %fusion.35), kind=kCustom, calls=%fused_computation.2.clone.1 | custom fusion | flops 1048576 | bytes 12583040 | tf_op jit(solution)/shard_map/while/body/eval_jaxpr/scatter-add | solution.py:42
  191.7 9.9 %scatter_fusion = f32[32,128,256]{2,1,0:T(8,128)} fusion(f32[32,128,256]{2,1,0:T(8,128)} %get-tuple-element.398, s32[32]{0:T(128)S(1)} %get-tuple-element.375, f32[32,128,256]{2,1,0:T(8,128)} %fusion.35), kind=kCustom, calls=%fused_computation.2.clone.1 | custom fusion | flops 1048576 | bytes 12583040 | tf_op jit(solution)/shard_map/while/body/eval_jaxpr/scatter-add | solution.py:42
  201.6 3.8 convert_element_type.63
  208.0 134.8 %while.27 = (s32[]{:T(128)}, f32[32,128,256]{2,1,0:T(8,128)}, s32[256]{0:T(256)S(1)}, s32[256,16,128]{2,1,0:T(8,128)}, s32[]{:T(128)}, /*index=5*/s32[256]{0:T(2...) while((s32[]{:T(128)}, f32[32,128,256]{2,1,0:T(8,128)}, ...), condition=%wide.region_7.8_spmd, body=%wide.region_5.7_spmd.sunk | while | flops 271582656 | bytes 23862704 | solution.py:46
  214.9 10.2 %scatter_fusion.1 = f32[32,128,256]{2,1,0:T(8,128)} fusion(f32[32,128,256]{2,1,0:T(8,128)} %get-tuple-element.431, s32[32]{0:T(128)S(1)} %get-tuple-element.384, f32[32,128,256]{2,1,0:T(8,128)} %fusion.38), kind=kCustom, calls=%fused_computation.3.clone.1 | custom fusion | flops 1048576 | bytes 12583040 | tf_op jit(solution)/shard_map/while/body/eval_jaxpr/scatter-add | solution.py:42
  232.0 9.8 %scatter_fusion.1 = f32[32,128,256]{2,1,0:T(8,128)} fusion(f32[32,128,256]{2,1,0:T(8,128)} %get-tuple-element.431, s32[32]{0:T(128)S(1)} %get-tuple-element.384, f32[32,128,256]{2,1,0:T(8,128)} %fusion.38), kind=kCustom, calls=%fused_computation.3.clone.1 | custom fusion | flops 1048576 | bytes 12583040 | tf_op jit(solution)/shard_map/while/body/eval_jaxpr/scatter-add | solution.py:42
  248.7 10.0 %scatter_fusion.1 = f32[32,128,256]{2,1,0:T(8,128)} fusion(f32[32,128,256]{2,1,0:T(8,128)} %get-tuple-element.431, s32[32]{0:T(128)S(1)} %get-tuple-element.384, f32[32,128,256]{2,1,0:T(8,128)} %fusion.38), kind=kCustom, calls=%fused_computation.3.clone.1 | custom fusion | flops 1048576 | bytes 12583040 | tf_op jit(solution)/shard_map/while/body/eval_jaxpr/scatter-add | solution.py:42
  265.5 9.9 %scatter_fusion.1 = f32[32,128,256]{2,1,0:T(8,128)} fusion(f32[32,128,256]{2,1,0:T(8,128)} %get-tuple-element.431, s32[32]{0:T(128)S(1)} %get-tuple-element.384, f32[32,128,256]{2,1,0:T(8,128)} %fusion.38), kind=kCustom, calls=%fused_computation.3.clone.1 | custom fusion | flops 1048576 | bytes 12583040 | tf_op jit(solution)/shard_map/while/body/eval_jaxpr/scatter-add | solution.py:42
  282.3 9.9 %scatter_fusion.1 = f32[32,128,256]{2,1,0:T(8,128)} fusion(f32[32,128,256]{2,1,0:T(8,128)} %get-tuple-element.431, s32[32]{0:T(128)S(1)} %get-tuple-element.384, f32[32,128,256]{2,1,0:T(8,128)} %fusion.38), kind=kCustom, calls=%fused_computation.3.clone.1 | custom fusion | flops 1048576 | bytes 12583040 | tf_op jit(solution)/shard_map/while/body/eval_jaxpr/scatter-add | solution.py:42
  299.0 10.0 %scatter_fusion.1 = f32[32,128,256]{2,1,0:T(8,128)} fusion(f32[32,128,256]{2,1,0:T(8,128)} %get-tuple-element.431, s32[32]{0:T(128)S(1)} %get-tuple-element.384, f32[32,128,256]{2,1,0:T(8,128)} %fusion.38), kind=kCustom, calls=%fused_computation.3.clone.1 | custom fusion | flops 1048576 | bytes 12583040 | tf_op jit(solution)/shard_map/while/body/eval_jaxpr/scatter-add | solution.py:42
  315.9 10.1 %scatter_fusion.1 = f32[32,128,256]{2,1,0:T(8,128)} fusion(f32[32,128,256]{2,1,0:T(8,128)} %get-tuple-element.431, s32[32]{0:T(128)S(1)} %get-tuple-element.384, f32[32,128,256]{2,1,0:T(8,128)} %fusion.38), kind=kCustom, calls=%fused_computation.3.clone.1 | custom fusion | flops 1048576 | bytes 12583040 | tf_op jit(solution)/shard_map/while/body/eval_jaxpr/scatter-add | solution.py:42
  332.8 10.0 %scatter_fusion.1 = f32[32,128,256]{2,1,0:T(8,128)} fusion(f32[32,128,256]{2,1,0:T(8,128)} %get-tuple-element.431, s32[32]{0:T(128)S(1)} %get-tuple-element.384, f32[32,128,256]{2,1,0:T(8,128)} %fusion.38), kind=kCustom, calls=%fused_computation.3.clone.1 | custom fusion | flops 1048576 | bytes 12583040 | tf_op jit(solution)/shard_map/while/body/eval_jaxpr/scatter-add | solution.py:42
  342.9 3.8 convert_element_type.71
  351.4 73.8 %reduce-scatter.5.cloned.1.call-done = bf16[256,256]{1,0:T(8,128)(2,1)} async-done(((bf16[4096,256]{1,0:T(8,128)(2,1)}), bf16[256,256]{1,0:T(8,128)(2,1)}) %reduce-scatter.5.cloned.1.call-update) | async-done | bytes 131088 | tf_op jit(solution)/shard_map/reduce_scatter | solution.py:77
  426.9 255.1 %all-reduce.2.cloned.1.call-done = f32[256,256]{1,0:T(8,128)} async-done(((f32[256,256]{1,0:T(8,128)}), f32[256,256]{1,0:T(8,128)}) %all-reduce.2.cloned.1.call-update) | async-done | bytes 262160 | tf_op jit(solution)/shard_map/psum | solution.py:98
  (155 shorter events, 124.4 us)
Async XLA Ops:
  7.2 342.4 %copy-start = (bf16[256,256]{1,0:T(8,128)(2,1)S(1)}, bf16[256,256]{1,0:T(8,128)(2,1)}, u32[]{:S(2)}) copy-start(bf16[256,256]{1,0:T(8,128)(2,1)} %param.15) | copy-start | bytes 393220
  7.2 55.9 %all-gather.3.cloned.1.call-start = ((), (), s32[]{:S(2)}) async-start(), calls=%async_computation.2 | async-start | bytes 2228224 | tf_op jit(solution)/shard_map/all_gather | solution.py:52
  7.9 197.6 %all-gather.5.cloned.1.call-start = ((), (), s32[]{:S(2)}) async-start(), calls=%async_computation.5 | async-start | bytes 2228224 | tf_op jit(solution)/shard_map/all_gather | solution.py:73
  10.3 336.5 %reduce-scatter.3.cloned.1.call-start = ((), (), s32[]{:S(2)}) async-start(), calls=%async_computation.3 | async-start | bytes 2228224 | tf_op jit(solution)/shard_map/reduce_scatter | solution.py:56
  63.1 2.5 copy-start.2
  63.1 2.5 copy-start.3
  205.5 219.7 %reduce-scatter.5.cloned.1.call-start = ((), (), s32[]{:S(2)}) async-start(), calls=%async_computation.6 | async-start | bytes 2228224 | tf_op jit(solution)/shard_map/reduce_scatter | solution.py:77
  346.7 0.9 copy-start.1
  346.7 335.2 %all-reduce.2.cloned.1.call-start = ((), (), s32[]{:S(2)}) async-start(), calls=%async_computation.4 | async-start | bytes 524288 | tf_op jit(solution)/shard_map/psum | solution.py:98
Sparse Core Ops, SparseCore 0:
  10.4 52.5 all-gather.2
  65.5 39.5 all-gather.4
  205.6 59.0 reduce-scatter.2
  346.9 78.2 reduce-scatter.4
  431.9 250.0 all-reduce.1
where the time goes:
time: 692 us; the launch traced here: 690 us
  waiting for transfers between devices  382 us (55%)
  other arithmetic  182 us (26%)
  local copies, waits for them, and re-layouts  60.8 us (9%)
  matrix products  50.3 us (7%)
  between operations  13.8 us (2%)
    psum x1, waiting for transfers between devices, per_device(): weight_grad = lax.psum(local_term, ('row', 'col'))  255 us
    scatter-add x16, other arithmetic, one_block(): return totals.at[placed].add(product)  159 us
    reduce_scatter x1, waiting for transfers between devices, backward_pass(): lax.psum_scatter(partial_value.reshape(-1, width).astype(jnp.bfloat16), '...  73.8 us
    all_gather x1, waiting for transfers between devices, forward_pass(): gathered = lax.all_gather(features, 'row', axis=0, tiled=True)  52.7 us
    dot_general x8, matrix products, one_block(): jnp.einsum('bji,bjf->bif', pattern, source[block_cols], preferred_element...  23.2 us
    dot_general x8, matrix products, one_block(): jnp.einsum('bji,bif->bjf', pattern, source[block_rows], preferred_element...  21.6 us
    gather x8, local copies, waits for them, and re-layouts, one_block(): source[block_rows]  18.2 us
    gather x8, local copies, waits for them, and re-layouts, one_block(): source[block_cols]  18.2 us
  transfers between devices with their start and end apart: 5, of which 3 were waited for; matrix products, arithmetic and copies ran while one was open for 42% of the time, Pallas kernels for 0%

commit v1 on v0

--- a/solution.py
+++ b/solution.py
@@ -95,7 +95,7 @@
     local_term = lax.dot_general(
         aggregated, cotangent, (((0,), (0,)), ((), ())), preferred_element_type=jnp.float32
     )
-    weight_grad = lax.psum(local_term, ("row", "col"))
+    weight_grad = lax.psum(lax.psum(local_term, "row"), "col")
     return (output, weight_grad, input_grad)
 
 

time: 692 us -> 645 us (0.932)
  waiting for transfers between devices: 382 us -> 336 us
    psum x1 -> x2, waiting for transfers between devices: 255 us -> 109 us  [per_device(): weight_grad = lax.psum(lax.psum(local_term, 'row'), 'col')]
    reduce_scatter x1, waiting for transfers between devices: 0.02 us -> 57.5 us  [forward_pass(): lax.psum_scatter(partial_value.reshape(-1, width).astype(jnp.bfloat16), '...]
    all_gather x1, waiting for transfers between devices: 0.02 us -> 38.7 us  [backward_pass(): gathered = lax.all_gather(scaled, 'col', axis=0, tiled=True)]
  transfers between devices with their start and end apart: 5 -> 6, of which waited for: 3 -> 5; matrix products, arithmetic and copies ran while one was open for 42% -> 23% of each run, Pallas kernels for 0% -> 0%
where the time goes in v1:
time: 645 us; the launch traced here: 643 us
  waiting for transfers between devices  336 us (52%)
  other arithmetic  181 us (28%)
  local copies, waits for them, and re-layouts  61.6 us (10%)
  matrix products  49.6 us (8%)
  between operations  14.1 us (2%)
    scatter-add x16, other arithmetic, one_block(): return totals.at[placed].add(product)  159 us
    psum x2, waiting for transfers between devices, per_device(): weight_grad = lax.psum(lax.psum(local_term, 'row'), 'col')  109 us
    reduce_scatter x1, waiting for transfers between devices, backward_pass(): lax.psum_scatter(partial_value.reshape(-1, width).astype(jnp.bfloat16), '...  75.7 us
    reduce_scatter x1, waiting for transfers between devices, forward_pass(): lax.psum_scatter(partial_value.reshape(-1, width).astype(jnp.bfloat16), '...  57.5 us
    all_gather x1, waiting for transfers between devices, forward_pass(): gathered = lax.all_gather(features, 'row', axis=0, tiled=True)  55.1 us
    all_gather x1, waiting for transfers between devices, backward_pass(): gathered = lax.all_gather(scaled, 'col', axis=0, tiled=True)  38.7 us
    dot_general x8, matrix products, one_block(): jnp.einsum('bji,bjf->bif', pattern, source[block_cols], preferred_element...  23.3 us
    dot_general x8, matrix products, one_block(): jnp.einsum('bji,bif->bjf', pattern, source[block_rows], preferred_element...  21.7 us
  transfers between devices with their start and end apart: 6, of which 5 were waited for; matrix products, arithmetic and copies ran while one was open for 23% of the time, Pallas kernels for 0%

profile of v1, /device:TPU:2, one launch (start us, length us, event | category | flops | bytes accessed | tf_op | source)
XLA Modules:
  0.0 642.8 jit_solution(17190796132954499026)
XLA Ops:
  8.0 55.1 %all-gather.3.cloned.1.call-done = bf16[4096,256]{1,0:T(8,128)(2,1)} async-done(((bf16[256,256]{1,0:T(8,128)(2,1)}), bf16[4096,256]{1,0:T(8,128)(2,1)}) %all-gather.3.cloned.1.call-update) | async-done | bytes 2097168 | tf_op jit(solution)/shard_map/all_gather | solution.py:52
  65.5 136.1 %while.26 = (s32[]{:T(128)}, f32[32,128,256]{2,1,0:T(8,128)}, s32[256]{0:T(256)S(1)}, s32[256,16,128]{2,1,0:T(8,128)}, s32[]{:T(128)}, /*index=5*/s32[256]{0:T(2...) while((s32[]{:T(128)}, f32[32,128,256]{2,1,0:T(8,128)}, ...), condition=%wide.region_2.3_spmd, body=%wide.region_0.2_spmd.sunk | while | flops 271582656 | bytes 23862704 | solution.py:46
  72.6 10.0 %scatter_fusion = f32[32,128,256]{2,1,0:T(8,128)} fusion(f32[32,128,256]{2,1,0:T(8,128)} %get-tuple-element.398, s32[32]{0:T(128)S(1)} %get-tuple-element.375, f32[32,128,256]{2,1,0:T(8,128)} %fusion.35), kind=kCustom, calls=%fused_computation.2.clone.1 | custom fusion | flops 1048576 | bytes 12583040 | tf_op jit(solution)/shard_map/while/body/eval_jaxpr/scatter-add | solution.py:42
  89.7 10.0 %scatter_fusion = f32[32,128,256]{2,1,0:T(8,128)} fusion(f32[32,128,256]{2,1,0:T(8,128)} %get-tuple-element.398, s32[32]{0:T(128)S(1)} %get-tuple-element.375, f32[32,128,256]{2,1,0:T(8,128)} %fusion.35), kind=kCustom, calls=%fused_computation.2.clone.1 | custom fusion | flops 1048576 | bytes 12583040 | tf_op jit(solution)/shard_map/while/body/eval_jaxpr/scatter-add | solution.py:42
  106.7 9.8 %scatter_fusion = f32[32,128,256]{2,1,0:T(8,128)} fusion(f32[32,128,256]{2,1,0:T(8,128)} %get-tuple-element.398, s32[32]{0:T(128)S(1)} %get-tuple-element.375, f32[32,128,256]{2,1,0:T(8,128)} %fusion.35), kind=kCustom, calls=%fused_computation.2.clone.1 | custom fusion | flops 1048576 | bytes 12583040 | tf_op jit(solution)/shard_map/while/body/eval_jaxpr/scatter-add | solution.py:42
  123.5 9.9 %scatter_fusion = f32[32,128,256]{2,1,0:T(8,128)} fusion(f32[32,128,256]{2,1,0:T(8,128)} %get-tuple-element.398, s32[32]{0:T(128)S(1)} %get-tuple-element.375, f32[32,128,256]{2,1,0:T(8,128)} %fusion.35), kind=kCustom, calls=%fused_computation.2.clone.1 | custom fusion | flops 1048576 | bytes 12583040 | tf_op jit(solution)/shard_map/while/body/eval_jaxpr/scatter-add | solution.py:42
  140.6 9.8 %scatter_fusion = f32[32,128,256]{2,1,0:T(8,128)} fusion(f32[32,128,256]{2,1,0:T(8,128)} %get-tuple-element.398, s32[32]{0:T(128)S(1)} %get-tuple-element.375, f32[32,128,256]{2,1,0:T(8,128)} %fusion.35), kind=kCustom, calls=%fused_computation.2.clone.1 | custom fusion | flops 1048576 | bytes 12583040 | tf_op jit(solution)/shard_map/while/body/eval_jaxpr/scatter-add | solution.py:42
  157.5 10.0 %scatter_fusion = f32[32,128,256]{2,1,0:T(8,128)} fusion(f32[32,128,256]{2,1,0:T(8,128)} %get-tuple-element.398, s32[32]{0:T(128)S(1)} %get-tuple-element.375, f32[32,128,256]{2,1,0:T(8,128)} %fusion.35), kind=kCustom, calls=%fused_computation.2.clone.1 | custom fusion | flops 1048576 | bytes 12583040 | tf_op jit(solution)/shard_map/while/body/eval_jaxpr/scatter-add | solution.py:42
  174.5 10.1 %scatter_fusion = f32[32,128,256]{2,1,0:T(8,128)} fusion(f32[32,128,256]{2,1,0:T(8,128)} %get-tuple-element.398, s32[32]{0:T(128)S(1)} %get-tuple-element.375, f32[32,128,256]{2,1,0:T(8,128)} %fusion.35), kind=kCustom, calls=%fused_computation.2.clone.1 | custom fusion | flops 1048576 | bytes 12583040 | tf_op jit(solution)/shard_map/while/body/eval_jaxpr/scatter-add | solution.py:42
  191.7 9.9 %scatter_fusion = f32[32,128,256]{2,1,0:T(8,128)} fusion(f32[32,128,256]{2,1,0:T(8,128)} %get-tuple-element.398, s32[32]{0:T(128)S(1)} %get-tuple-element.375, f32[32,128,256]{2,1,0:T(8,128)} %fusion.35), kind=kCustom, calls=%fused_computation.2.clone.1 | custom fusion | flops 1048576 | bytes 12583040 | tf_op jit(solution)/shard_map/while/body/eval_jaxpr/scatter-add | solution.py:42
  201.6 3.8 convert_element_type.63
  207.2 57.5 %reduce-scatter.3.cloned.1.call-done = bf16[256,256]{1,0:T(8,128)(2,1)} async-done(((bf16[4096,256]{1,0:T(8,128)(2,1)}), bf16[256,256]{1,0:T(8,128)(2,1)}) %reduce-scatter.3.cloned.1.call-update) | async-done | bytes 131088 | tf_op jit(solution)/shard_map/reduce_scatter | solution.py:56
  266.6 38.7 %all-gather.5.cloned.1.call-done = bf16[4096,256]{1,0:T(8,128)(2,1)} async-done(((bf16[256,256]{1,0:T(8,128)(2,1)}), bf16[4096,256]{1,0:T(8,128)(2,1)}) %all-gather.5.cloned.1.call-update) | async-done | bytes 2097168 | tf_op jit(solution)/shard_map/all_gather | solution.py:73
  307.8 134.8 %while.27 = (s32[]{:T(128)}, f32[32,128,256]{2,1,0:T(8,128)}, s32[256]{0:T(256)S(1)}, s32[256,16,128]{2,1,0:T(8,128)}, s32[]{:T(128)}, /*index=5*/s32[256]{0:T(2...) while((s32[]{:T(128)}, f32[32,128,256]{2,1,0:T(8,128)}, ...), condition=%wide.region_8.9_spmd, body=%wide.region_6.0_spmd.sunk | while | flops 271582656 | bytes 23862704 | solution.py:46
  314.6 10.1 %scatter_fusion.1 = f32[32,128,256]{2,1,0:T(8,128)} fusion(f32[32,128,256]{2,1,0:T(8,128)} %get-tuple-element.431, s32[32]{0:T(128)S(1)} %get-tuple-element.384, f32[32,128,256]{2,1,0:T(8,128)} %fusion.38), kind=kCustom, calls=%fused_computation.3.clone.1 | custom fusion | flops 1048576 | bytes 12583040 | tf_op jit(solution)/shard_map/while/body/eval_jaxpr/scatter-add | solution.py:42
  331.7 9.8 %scatter_fusion.1 = f32[32,128,256]{2,1,0:T(8,128)} fusion(f32[32,128,256]{2,1,0:T(8,128)} %get-tuple-element.431, s32[32]{0:T(128)S(1)} %get-tuple-element.384, f32[32,128,256]{2,1,0:T(8,128)} %fusion.38), kind=kCustom, calls=%fused_computation.3.clone.1 | custom fusion | flops 1048576 | bytes 12583040 | tf_op jit(solution)/shard_map/while/body/eval_jaxpr/scatter-add | solution.py:42
  348.3 9.9 %scatter_fusion.1 = f32[32,128,256]{2,1,0:T(8,128)} fusion(f32[32,128,256]{2,1,0:T(8,128)} %get-tuple-element.431, s32[32]{0:T(128)S(1)} %get-tuple-element.384, f32[32,128,256]{2,1,0:T(8,128)} %fusion.38), kind=kCustom, calls=%fused_computation.3.clone.1 | custom fusion | flops 1048576 | bytes 12583040 | tf_op jit(solution)/shard_map/while/body/eval_jaxpr/scatter-add | solution.py:42
  365.1 9.9 %scatter_fusion.1 = f32[32,128,256]{2,1,0:T(8,128)} fusion(f32[32,128,256]{2,1,0:T(8,128)} %get-tuple-element.431, s32[32]{0:T(128)S(1)} %get-tuple-element.384, f32[32,128,256]{2,1,0:T(8,128)} %fusion.38), kind=kCustom, calls=%fused_computation.3.clone.1 | custom fusion | flops 1048576 | bytes 12583040 | tf_op jit(solution)/shard_map/while/body/eval_jaxpr/scatter-add | solution.py:42
  381.9 9.9 %scatter_fusion.1 = f32[32,128,256]{2,1,0:T(8,128)} fusion(f32[32,128,256]{2,1,0:T(8,128)} %get-tuple-element.431, s32[32]{0:T(128)S(1)} %get-tuple-element.384, f32[32,128,256]{2,1,0:T(8,128)} %fusion.38), kind=kCustom, calls=%fused_computation.3.clone.1 | custom fusion | flops 1048576 | bytes 12583040 | tf_op jit(solution)/shard_map/while/body/eval_jaxpr/scatter-add | solution.py:42
  398.7 10.1 %scatter_fusion.1 = f32[32,128,256]{2,1,0:T(8,128)} fusion(f32[32,128,256]{2,1,0:T(8,128)} %get-tuple-element.431, s32[32]{0:T(128)S(1)} %get-tuple-element.384, f32[32,128,256]{2,1,0:T(8,128)} %fusion.38), kind=kCustom, calls=%fused_computation.3.clone.1 | custom fusion | flops 1048576 | bytes 12583040 | tf_op jit(solution)/shard_map/while/body/eval_jaxpr/scatter-add | solution.py:42
  415.6 10.1 %scatter_fusion.1 = f32[32,128,256]{2,1,0:T(8,128)} fusion(f32[32,128,256]{2,1,0:T(8,128)} %get-tuple-element.431, s32[32]{0:T(128)S(1)} %get-tuple-element.384, f32[32,128,256]{2,1,0:T(8,128)} %fusion.38), kind=kCustom, calls=%fused_computation.3.clone.1 | custom fusion | flops 1048576 | bytes 12583040 | tf_op jit(solution)/shard_map/while/body/eval_jaxpr/scatter-add | solution.py:42
  432.5 10.0 %scatter_fusion.1 = f32[32,128,256]{2,1,0:T(8,128)} fusion(f32[32,128,256]{2,1,0:T(8,128)} %get-tuple-element.431, s32[32]{0:T(128)S(1)} %get-tuple-element.384, f32[32,128,256]{2,1,0:T(8,128)} %fusion.38), kind=kCustom, calls=%fused_computation.3.clone.1 | custom fusion | flops 1048576 | bytes 12583040 | tf_op jit(solution)/shard_map/while/body/eval_jaxpr/scatter-add | solution.py:42
  448.2 75.7 %reduce-scatter.5.cloned.1.call-done = bf16[256,256]{1,0:T(8,128)(2,1)} async-done(((bf16[4096,256]{1,0:T(8,128)(2,1)}), bf16[256,256]{1,0:T(8,128)(2,1)}) %reduce-scatter.5.cloned.1.call-update) | async-done | bytes 131088 | tf_op jit(solution)/shard_map/reduce_scatter | solution.py:77
  525.7 108.6 %all-reduce.5.cloned.1.call-done = f32[256,256]{1,0:T(8,128)} async-done(((f32[256,256]{1,0:T(8,128)}), f32[256,256]{1,0:T(8,128)}) %all-reduce.5.cloned.1.call-update) | async-done | bytes 262160 | tf_op jit(solution)/shard_map/psum | solution.py:98
  (162 shorter events, 129.7 us)
Async XLA Ops:
  7.2 439.3 %copy-start = (bf16[256,256]{1,0:T(8,128)(2,1)S(1)}, bf16[256,256]{1,0:T(8,128)(2,1)}, u32[]{:S(2)}) copy-start(bf16[256,256]{1,0:T(8,128)(2,1)} %param.15) | copy-start | bytes 393220
  7.2 55.9 %all-gather.3.cloned.1.call-start = ((), (), s32[]{:S(2)}) async-start(), calls=%async_computation.2 | async-start | bytes 2228224 | tf_op jit(solution)/shard_map/all_gather | solution.py:52
  7.9 256.7 %reduce-scatter.3.cloned.1.call-start = ((), (), s32[]{:S(2)}) async-start(), calls=%async_computation.3 | async-start | bytes 2228224 | tf_op jit(solution)/shard_map/reduce_scatter | solution.py:56
  63.1 2.5 copy-start.2
  63.1 2.5 copy-start.3
  205.4 0.7 copy-start.4
  205.4 0.9 copy-start.1
  205.5 99.9 %all-gather.5.cloned.1.call-start = ((), (), s32[]{:S(2)}) async-start(), calls=%async_computation.6 | async-start | bytes 2228224 | tf_op jit(solution)/shard_map/all_gather | solution.py:73
  207.1 241.0 %all-reduce.3.cloned.1.call-start = ((), (), s32[]{:S(2)}) async-start(), calls=%async_computation.4 | async-start | bytes 524288 | tf_op jit(solution)/shard_map/psum | solution.py:98
  266.6 257.3 %reduce-scatter.5.cloned.1.call-start = ((), (), s32[]{:S(2)}) async-start(), calls=%async_computation.7 | async-start | bytes 2228224 | tf_op jit(solution)/shard_map/reduce_scatter | solution.py:77
  446.4 0.9 copy-start.5
  446.4 187.9 %all-reduce.5.cloned.1.call-start = ((), (), s32[]{:S(2)}) async-start(), calls=%async_computation.5 | async-start | bytes 524288 | tf_op jit(solution)/shard_map/psum | solution.py:98
Sparse Core Ops, SparseCore 0:
  10.4 52.5 all-gather.2
  205.6 59.0 reduce-scatter.2
  267.1 38.2 all-gather.4
  308.9 92.3 all-reduce.2
  446.5 77.3 reduce-scatter.4
  526.1 108.1 all-reduce.4
